TPU v7x, 32 devices: a whole 2x2x4 slice. The times are simulated.
32 devices in a mesh: groups: 2 (over y), scanx: 4 (over z), scany: 2 (over x), pos: 2 (over core).
Axes of the slice: x: 2, y: 2, z: 4, core: 2. Of those that a mesh axis runs over, the one named last changes fastest.
Arguments:
- specimen: float32 [2, 2048, 512], P(None, ('groups', 'scanx'), 'scany'), parts along dimension 1, may hold values from -5 to 5
- probe_wave: float32 [2, 512, 256], P(None, 'groups'), parts along dimension 1, may hold values from -6 to 6
- amplitudes: bfloat16 [64, 256, 256], P(('groups', 'scanx', 'scany', 'pos')), parts along dimension 0, may hold values from 0 to 2
- offsets: int32 [64, 2], P(('groups', 'scanx', 'scany', 'pos')), parts along dimension 0, may hold values from 0 to 255
Outputs:
- new_specimen: float32 [2, 2048, 512], P(None, ('groups', 'scanx'), 'scany'), parts along dimension 1
- new_probe: float32 [2, 512, 256], P(None, 'groups'), parts along dimension 1
There are 2 independent parts, one for each index of `groups`. A program takes and returns all parts, laid end to end along the dimension named above; each array names one. Nothing has to cross between parts.
Inputs may be any that keep to these rules, and one draw needn't show every extreme that they name: offsets are pixels from the top-left corner of the position's tile.
All inputs are finite; a program needn't handle non-finite values.
Results may differ from a plain program's by a relative error of at most 0.002.
The roundings to bfloat16 on the way count: a program that leaves them out, or rounds other values in their place, can miss the bound.
Values sent between devices are 32-bit elements; how exact they have to be, the bound alone decides.
A program may use at most 64 MiB of HBM per device.

v0:
```python
import math
import jax
import jax.numpy as jnp
from jax import lax
from jax.sharding import PartitionSpec as P


def padded_2(block, sides, width):
    for axis, dim in sides:
        count = lax.axis_size(axis)
        forward = [(i, i + 1) for i in range(count - 1)]
        backward = [(target, source) for source, target in forward]
        low = lax.ppermute(
            lax.slice_in_dim(block, block.shape[dim] - width, None, axis=dim), axis, forward
        )
        high = lax.ppermute(lax.slice_in_dim(block, 0, width, axis=dim), axis, backward)
        block = jnp.concatenate([low, block, high], axis=dim)
    return block


def dft_tables(length):
    positions_index = jnp.arange(length, dtype=jnp.int32)
    phase_index = positions_index[:, None] * positions_index[None, :] % length
    angle_rad = phase_index.astype(jnp.float32) * (2.0 * math.pi / length)
    scale_factor = 1.0 / math.sqrt(length)
    cosine = (jnp.cos(angle_rad) * scale_factor).astype(jnp.bfloat16)
    sine_part = (jnp.sin(angle_rad) * scale_factor).astype(jnp.bfloat16)
    forward_left = jnp.stack(
        [jnp.stack([cosine, sine_part], 1), jnp.stack([-sine_part, cosine], 1)], 0
    )
    forward_right = jnp.stack(
        [jnp.stack([cosine, -sine_part], 1), jnp.stack([sine_part, cosine], 1)], 0
    )
    inverse_left = jnp.stack(
        [jnp.stack([cosine, -sine_part], 1), jnp.stack([sine_part, cosine], 1)], 0
    )
    inverse_right = jnp.stack(
        [jnp.stack([cosine, sine_part], 1), jnp.stack([-sine_part, cosine], 1)], 0
    )
    return (forward_left, forward_right, inverse_left, inverse_right)


def project_exit(patch_wave, probe_real, probe_imag, amplitude, tables):
    forward_left, forward_right, inverse_left, inverse_right = tables
    patch_real = patch_wave[0]
    patch_imag = patch_wave[1]
    exit_real = probe_real * patch_real - probe_imag * patch_imag
    exit_imag = probe_real * patch_imag + probe_imag * patch_real
    exit_wave = jnp.stack([exit_real, exit_imag]).astype(jnp.bfloat16)
    half_done = jnp.einsum(
        "akbr,brv->akv", forward_left, exit_wave, preferred_element_type=jnp.float32
    ).astype(jnp.bfloat16)
    far_field = jnp.einsum(
        "bkv,bval->akl", half_done, forward_right, preferred_element_type=jnp.float32
    )
    magnitude = jnp.sqrt(far_field[0] * far_field[0] + far_field[1] * far_field[1])
    scale_ratio = amplitude.astype(jnp.float32) / jnp.maximum(magnitude, 0.2)
    projected = (far_field * scale_ratio[None]).astype(jnp.bfloat16)
    back_half = jnp.einsum(
        "akbr,brv->akv", inverse_left, projected, preferred_element_type=jnp.float32
    ).astype(jnp.bfloat16)
    back_wave = jnp.einsum(
        "bkv,bval->akl", back_half, inverse_right, preferred_element_type=jnp.float32
    )
    return (back_wave[0] - exit_real, back_wave[1] - exit_imag, patch_real, patch_imag)


def fold_margin(field_in, axis_dim, margin, tile_len):
    extent = field_in.shape[axis_dim]
    inner_part = lax.slice_in_dim(field_in, 2 * margin, 2 * margin + tile_len, axis=axis_dim)
    lower_rim = lax.slice_in_dim(field_in, 0, margin, axis=axis_dim)
    upper_rim = lax.slice_in_dim(field_in, extent - margin, extent, axis=axis_dim)
    lower_widths = [(0, 0)] * field_in.ndim
    upper_widths = [(0, 0)] * field_in.ndim
    lower_widths[axis_dim] = (0, tile_len - margin)
    upper_widths[axis_dim] = (tile_len - margin, 0)
    return inner_part + jnp.pad(lower_rim, lower_widths) + jnp.pad(upper_rim, upper_widths)


def shards(specimen, probe_wave, amplitudes, offsets):
    pattern = probe_wave.shape[1]
    margin = pattern // 2
    tile_len = specimen.shape[1]
    tables = dft_tables(pattern)
    padded = padded_2(specimen, (("scanx", 1), ("scany", 2)), margin)
    probe_real = probe_wave[0]
    probe_imag = probe_wave[1]
    probe_power = probe_real * probe_real + probe_imag * probe_imag
    zero_index = jnp.zeros((), jnp.int32)

    def visit_position(carried, inputs):
        object_grad, probe_grad = carried
        amplitude, offset = inputs
        row_start = offset[0]
        col_start = offset[1]
        patch_wave = lax.dynamic_slice(
            padded, (zero_index, row_start, col_start), (2, pattern, pattern)
        )
        diff_real, diff_imag, patch_real, patch_imag = project_exit(
            patch_wave, probe_real, probe_imag, amplitude, tables
        )
        object_term = jnp.stack(
            [
                probe_real * diff_real + probe_imag * diff_imag,
                probe_real * diff_imag - probe_imag * diff_real,
                probe_power,
            ]
        )
        current = lax.dynamic_slice(
            object_grad, (zero_index, row_start, col_start), (3, pattern, pattern)
        )
        object_grad = lax.dynamic_update_slice(
            object_grad, current + object_term, (zero_index, row_start, col_start)
        )
        probe_term = jnp.stack(
            [
                patch_real * diff_real + patch_imag * diff_imag,
                patch_real * diff_imag - patch_imag * diff_real,
            ]
        )
        return ((object_grad, probe_grad + probe_term), None)

    start_grad = jnp.zeros((3, tile_len + pattern, tile_len + pattern), jnp.float32)
    start_probe = jnp.zeros((2, pattern, pattern), jnp.float32)
    (object_grad, probe_grad), unused = lax.scan(
        visit_position, (start_grad, start_probe), (amplitudes, offsets)
    )
    row_halo = padded_2(object_grad, (("scanx", 1),), margin)
    row_folded = fold_margin(row_halo, 1, margin, tile_len)
    col_halo = padded_2(row_folded, (("scany", 2),), margin)
    core_sum = fold_margin(col_halo, 2, margin, tile_len)
    core_sum = lax.psum(core_sum, "pos")
    new_specimen = specimen + core_sum[0:2] / (core_sum[2:3] + 1.0)
    devices_count = lax.axis_size("scanx") * lax.axis_size("scany") * lax.axis_size("pos")
    step_size = 1.0 / math.sqrt(offsets.shape[0] * devices_count)
    total_grad = lax.psum(probe_grad, ("scanx", "scany", "pos"))
    new_probe = probe_wave + total_grad * step_size
    return (new_specimen, new_probe)


def solution(mesh):
    placed = (
        P(None, ("groups", "scanx"), "scany"),
        P(None, "groups", None),
        P(("groups", "scanx", "scany", "pos"), None, None),
        P(("groups", "scanx", "scany", "pos"), None),
    )
    return jax.shard_map(
        shards,
        mesh=mesh,
        in_specs=placed,
        out_specs=(P(None, ("groups", "scanx"), "scany"), P(None, "groups", None)),
        check_vma=False,
    )
```

profile of v0, /device:TPU:0, one launch (start us, length us, event | category | flops | bytes accessed | tf_op | source)
XLA Modules:
  0.0 249.2 jit_solution(168859406196740415)
XLA Ops:
  9.6 5.6 %collective-permute-start = (f32[2,128,256]{2,1,0:T(8,128)S(1)}, f32[2,128,256]{2,1,0:T(8,128)S(1)}, u32[]{:S(2)}, u32[]{:S(2)}) collective-permute-start(f32[2,128,256]{2,1,0:T(8,128)S(1)} %get-tuple-element.187), channel_id=1, source_target_pairs={{0,4},{4,8},{8,12},{1,5},{5,9},{9,13},{2,6},{6,10},{10,14},{3,7},{... | collective-permute-start | bytes 786440 | tf_op jit(solution)/shard_map/ppermute | solution.py:13
  18.3 2.5 collective-permute-done
  21.8 4.4 %collective-permute-start.2 = (f32[2,512,128]{2,1,0:T(8,128)}, f32[2,512,128]{2,1,0:T(8,128)}, u32[]{:S(2)}, u32[]{:S(2)}) collective-permute-start(f32[2,512,128]{2,1,0:T(8,128)} %get-tuple-element.182), channel_id=1, source_target_pairs={{0,2},{1,3},{4,6},{5,7},{8,10},{9,11},{12,14},{13,15},{16,18},{17,... | collective-permute-start | bytes 1572872 | tf_op jit(solution)/shard_map/ppermute | solution.py:13
  29.8 5.9 %collective-permute-done.2 = f32[2,512,128]{2,1,0:T(8,128)} collective-permute-done((f32[2,512,128]{2,1,0:T(8,128)}, f32[2,512,128]{2,1,0:T(8,128)}, u32[]{:S(2)}, u32[]{:S(2)}) %collective-permute-start.2) | collective-permute-done | bytes 524320 | tf_op jit(solution)/shard_map/ppermute | solution.py:13
  35.7 4.7 %collective-permute-done.3 = f32[2,512,128]{2,1,0:T(8,128)} collective-permute-done((f32[2,512,128]{2,1,0:T(8,128)S(1)}, f32[2,512,128]{2,1,0:T(8,128)}, u32[]{:S(2)}, u32[]{:S(2)}) %collective-permute-start.3) | collective-permute-done | bytes 524320 | tf_op jit(solution)/shard_map/ppermute | solution.py:16
  41.8 2.0 broadcast_in_dim.10
  43.8 53.8 %while.14 = (s32[]{:T(128)}, f32[3,512,512]{2,1,0:T(8,128)}, f32[2,256,256]{2,1,0:T(8,128)}, s32[2,2]{1,0:T(2,128)S(1)}, f32[256,256]{1,0:T(8,128)}, /*index=5*/...) while((s32[]{:T(128)}, f32[3,512,512]{2,1,0:T(8,128)}, ...), condition=%wide.region_1.2_spmd.clone, body=%wide.region_0.1_spmd.clone.sunk | while | flops 540737536 | bytes 17170760 | solution.py:125
  48.2 2.0 fusion.72
  53.8 2.0 convolution_bitcast_fusion.7
  60.8 9.5 %dynamic_update_slice.6 = f32[3,512,512]{2,1,0:T(8,128)} dynamic-update-slice(f32[3,512,512]{2,1,0:T(8,128)} %get-tuple-element.303, f32[3,256,256]{2,1,0:T(8,128)S(1)} %maximum_add_fusion.4, s32[]{:T(128)} %constant.39.clone.1..sunk, s32[]{:T(128)S(6)} %select_n.64, s32[]{:T(128)S(6)} %select_n.65) | dynamic-update-slice | bytes 1572868 | tf_op jit(solution)/shard_map/while/body/eval_jaxpr/dynamic_update_slice | solution.py:112
  74.6 2.0 fusion.72
  76.6 1.9 convolution_bitcast_fusion.6
  80.2 2.0 convolution_bitcast_fusion.7
  84.7 1.9 maximum_add_fusion.5
  88.2 9.4 %dynamic_update_slice.6 = f32[3,512,512]{2,1,0:T(8,128)} dynamic-update-slice(f32[3,512,512]{2,1,0:T(8,128)} %get-tuple-element.303, f32[3,256,256]{2,1,0:T(8,128)S(1)} %maximum_add_fusion.4, s32[]{:T(128)} %constant.39.clone.1..sunk, s32[]{:T(128)S(6)} %select_n.64, s32[]{:T(128)S(6)} %select_n.65) | dynamic-update-slice | bytes 1572868 | tf_op jit(solution)/shard_map/while/body/eval_jaxpr/dynamic_update_slice | solution.py:112
  99.3 3.0 %collective-permute-start.4 = (f32[3,128,512]{2,1,0:T(8,128)S(1)}, f32[3,128,512]{2,1,0:T(8,128)S(1)}, u32[]{:S(2)}, u32[]{:S(2)}) collective-permute-start(f32[3,128,512]{2,1,0:T(8,128)S(1)} %get-tuple-element.178), channel_id=1, source_target_pairs={{0,4},{4,8},{8,12},{1,5},{5,9},{9,13},{2,6},{6,10},{10,14},{3,7},{... | collective-permute-start | bytes 2359304 | tf_op jit(solution)/shard_map/ppermute | solution.py:13
  103.5 14.3 %collective-permute-done.4 = f32[3,128,512]{2,1,0:T(8,128)S(1)} collective-permute-done((f32[3,128,512]{2,1,0:T(8,128)S(1)}, f32[3,128,512]{2,1,0:T(8,128)S(1)}, u32[]{:S(2)}, u32[]{:S(2)}) %collective-permute-start.4) | collective-permute-done | bytes 786464 | tf_op jit(solution)/shard_map/ppermute | solution.py:13
  117.8 4.2 %collective-permute-done.5 = f32[3,128,512]{2,1,0:T(8,128)S(1)} collective-permute-done((f32[3,128,512]{2,1,0:T(8,128)S(1)}, f32[3,128,512]{2,1,0:T(8,128)S(1)}, u32[]{:S(2)}, u32[]{:S(2)}) %collective-permute-start.5) | collective-permute-done | bytes 786464 | tf_op jit(solution)/shard_map/ppermute | solution.py:16
  126.2 4.3 %collective-permute-done.6 = f32[3,256,128]{2,1,0:T(8,128)S(1)} collective-permute-done((f32[3,256,128]{2,1,0:T(8,128)}, f32[3,256,128]{2,1,0:T(8,128)S(1)}, u32[]{:S(2)}, u32[]{:S(2)}) %collective-permute-start.6) | collective-permute-done | bytes 393248 | tf_op jit(solution)/shard_map/ppermute | solution.py:13
  130.5 4.7 %collective-permute-done.7 = f32[3,256,128]{2,1,0:T(8,128)S(1)} collective-permute-done((f32[3,256,128]{2,1,0:T(8,128)}, f32[3,256,128]{2,1,0:T(8,128)S(1)}, u32[]{:S(2)}, u32[]{:S(2)}) %collective-permute-start.7) | collective-permute-done | bytes 393248 | tf_op jit(solution)/shard_map/ppermute | solution.py:16
  136.4 81.3 %all-reduce.9.cloned.1.call-done = f32[2,256,256]{2,1,0:T(8,128)} async-done(((f32[2,256,256]{2,1,0:T(8,128)}), f32[2,256,256]{2,1,0:T(8,128)}) %all-reduce.9.cloned.1.call-update) | async-done | bytes 524304 | tf_op jit(solution)/shard_map/psum | solution.py:136
  217.6 1.9 multiply_add_fusion.1
  219.5 19.9 %all-reduce.7.cloned.1.call-done = f32[3,256,256]{2,1,0:T(8,128)} async-done(((f32[3,256,256]{2,1,0:T(8,128)}), f32[3,256,256]{2,1,0:T(8,128)}) %all-reduce.7.cloned.1.call-update) | async-done | bytes 786448 | tf_op jit(solution)/shard_map/psum | solution.py:132
  240.4 1.9 fusion.29
  (56 shorter events, 36.4 us)
Async XLA Ops:
  7.2 13.6 %copy-start.3 = (f32[2,256,256]{2,1,0:T(8,128)S(1)}, f32[2,256,256]{2,1,0:T(8,128)}, u32[]{:S(2)}) copy-start(f32[2,256,256]{2,1,0:T(8,128)} %param.6) | copy-start | bytes 1572868
  7.2 210.5 %all-reduce.9.cloned.1.call-start = ((), (), s32[]{:S(2)}) async-start(), calls=%async_computation.1 | async-start | bytes 1048576 | tf_op jit(solution)/shard_map/psum | solution.py:136
  8.3 12.5 %collective-permute-start.1 = (f32[2,128,256]{2,1,0:T(8,128)S(1)}, f32[2,128,256]{2,1,0:T(8,128)S(1)}, u32[]{:S(2)}, u32[]{:S(2)}) collective-permute-start(f32[2,128,256]{2,1,0:T(8,128)S(1)} %get-tuple-element.186), channel_id=1, source_target_pairs={{4,0},{8,4},{12,8},{5,1},{9,5},{13,9},{6,2},{10,6},{14,10},{7,3},{... | collective-permute-start | bytes 786440 | tf_op jit(solution)/shard_map/ppermute | solution.py:16
  9.6 11.1 %collective-permute-start = (f32[2,128,256]{2,1,0:T(8,128)S(1)}, f32[2,128,256]{2,1,0:T(8,128)S(1)}, u32[]{:S(2)}, u32[]{:S(2)}) collective-permute-start(f32[2,128,256]{2,1,0:T(8,128)S(1)} %get-tuple-element.187), channel_id=1, source_target_pairs={{0,4},{4,8},{8,12},{1,5},{5,9},{9,13},{2,6},{6,10},{10,14},{3,7},{... | collective-permute-start | bytes 786440 | tf_op jit(solution)/shard_map/ppermute | solution.py:13
  20.9 7.4 %copy-start.1 = (f32[2,256,256]{2,1,0:T(8,128)S(1)}, f32[2,256,256]{2,1,0:T(8,128)}, u32[]{:S(2)}) copy-start(f32[2,256,256]{2,1,0:T(8,128)} %param.7) | copy-start | bytes 1572868
  21.8 13.9 %collective-permute-start.2 = (f32[2,512,128]{2,1,0:T(8,128)}, f32[2,512,128]{2,1,0:T(8,128)}, u32[]{:S(2)}, u32[]{:S(2)}) collective-permute-start(f32[2,512,128]{2,1,0:T(8,128)} %get-tuple-element.182), channel_id=1, source_target_pairs={{0,2},{1,3},{4,6},{5,7},{8,10},{9,11},{12,14},{13,15},{16,18},{17,... | collective-permute-start | bytes 1572872 | tf_op jit(solution)/shard_map/ppermute | solution.py:13
  26.1 14.2 %collective-permute-start.3 = (f32[2,512,128]{2,1,0:T(8,128)S(1)}, f32[2,512,128]{2,1,0:T(8,128)}, u32[]{:S(2)}, u32[]{:S(2)}) collective-permute-start(f32[2,512,128]{2,1,0:T(8,128)S(1)} %get-tuple-element.183), channel_id=1, source_target_pairs={{2,0},{3,1},{6,4},{7,5},{10,8},{11,9},{14,12},{15,13},{18,16},{19,... | collective-permute-start | bytes 1572872 | tf_op jit(solution)/shard_map/ppermute | solution.py:16
  41.8 2.0 copy-start.5
  97.6 24.3 %copy-start = (f32[3,512,512]{2,1,0:T(8,128)S(1)}, f32[3,512,512]{2,1,0:T(8,128)}, u32[]{:S(2)}) copy-start(f32[3,512,512]{2,1,0:T(8,128)} %get-tuple-element.93) | copy-start | bytes 9437188
  99.3 18.5 %collective-permute-start.4 = (f32[3,128,512]{2,1,0:T(8,128)S(1)}, f32[3,128,512]{2,1,0:T(8,128)S(1)}, u32[]{:S(2)}, u32[]{:S(2)}) collective-permute-start(f32[3,128,512]{2,1,0:T(8,128)S(1)} %get-tuple-element.178), channel_id=1, source_target_pairs={{0,4},{4,8},{8,12},{1,5},{5,9},{9,13},{2,6},{6,10},{10,14},{3,7},{... | collective-permute-start | bytes 2359304 | tf_op jit(solution)/shard_map/ppermute | solution.py:13
  102.2 19.7 %collective-permute-start.5 = (f32[3,128,512]{2,1,0:T(8,128)S(1)}, f32[3,128,512]{2,1,0:T(8,128)S(1)}, u32[]{:S(2)}, u32[]{:S(2)}) collective-permute-start(f32[3,128,512]{2,1,0:T(8,128)S(1)} %get-tuple-element.179), channel_id=1, source_target_pairs={{4,0},{8,4},{12,8},{5,1},{9,5},{13,9},{6,2},{10,6},{14,10},{7,3},{... | collective-permute-start | bytes 2359304 | tf_op jit(solution)/shard_map/ppermute | solution.py:16
  123.2 94.4 %copy-start.2 = (f32[2,256,256]{2,1,0:T(8,128)S(1)}, f32[2,256,256]{2,1,0:T(8,128)}, u32[]{:S(2)}) copy-start(f32[2,256,256]{2,1,0:T(8,128)} %param.7) | copy-start | bytes 1572868
  123.2 7.3 %collective-permute-start.6 = (f32[3,256,128]{2,1,0:T(8,128)}, f32[3,256,128]{2,1,0:T(8,128)S(1)}, u32[]{:S(2)}, u32[]{:S(2)}) collective-permute-start(f32[3,256,128]{2,1,0:T(8,128)} %get-tuple-element.180), channel_id=1, source_target_pairs={{0,2},{1,3},{4,6},{5,7},{8,10},{9,11},{12,14},{13,15},{16,18},{17,... | collective-permute-start | bytes 1179656 | tf_op jit(solution)/shard_map/ppermute | solution.py:13
  124.9 10.4 %collective-permute-start.7 = (f32[3,256,128]{2,1,0:T(8,128)}, f32[3,256,128]{2,1,0:T(8,128)S(1)}, u32[]{:S(2)}, u32[]{:S(2)}) collective-permute-start(f32[3,256,128]{2,1,0:T(8,128)} %get-tuple-element.181), channel_id=1, source_target_pairs={{2,0},{3,1},{6,4},{7,5},{10,8},{11,9},{14,12},{15,13},{18,16},{19,... | collective-permute-start | bytes 1179656 | tf_op jit(solution)/shard_map/ppermute | solution.py:16
  126.2 114.2 %copy-start.4 = (f32[2,256,256]{2,1,0:T(8,128)S(1)}, f32[2,256,256]{2,1,0:T(8,128)}, u32[]{:S(2)}) copy-start(f32[2,256,256]{2,1,0:T(8,128)} %param.6) | copy-start | bytes 1572868
  126.2 113.2 %all-reduce.7.cloned.1.call-start = ((), (), s32[]{:S(2)}) async-start(), calls=%async_computation | async-start | bytes 1572864 | tf_op jit(solution)/shard_map/psum | solution.py:132
Sparse Core Ops, SparseCore 0:
  126.3 91.2 all-reduce.8
  220.0 19.4 all-reduce.6
where the time goes:
time: 251 us; the launch traced here: 249 us
  waiting for transfers between devices  142 us (57%)
  other arithmetic  29.9 us (12%)
  local copies, waits for them, and re-layouts  28.3 us (11%)
  starting transfers between devices  19.8 us (8%)
  between operations  14.2 us (6%)
  matrix products  7.75 us (3%)
  loops' own time  7.59 us (3%)
    psum x1, waiting for transfers between devices, shards(): total_grad = lax.psum(probe_grad, ('scanx', 'scany', 'pos'))  81.3 us
    ppermute x4, waiting for transfers between devices, padded_2(): lax.ppermute(lax.slice_in_dim(block, block.shape[dim] - width, None, axis...  26.9 us
    psum x1, waiting for transfers between devices, shards(): core_sum = lax.psum(core_sum, 'pos')  19.9 us
    dynamic_update_slice x2, local copies, waits for them, and re-layouts, visit_position(): lax.dynamic_update_slice(object_grad, current + object_term, (zero_index,...  18.8 us
    ppermute x4, starting transfers between devices, padded_2(): lax.ppermute(lax.slice_in_dim(block, block.shape[dim] - width, None, axis...  14.5 us
    ppermute x4, waiting for transfers between devices, padded_2(): lax.ppermute(lax.slice_in_dim(block, 0, width, axis=dim), axis, backward)  13.6 us
    another operation x1, loops' own time, shards(): lax.scan(visit_position, (start_grad, start_probe), (amplitudes, offsets))  7.59 us
    ppermute x4, starting transfers between devices, padded_2(): lax.ppermute(lax.slice_in_dim(block, 0, width, axis=dim), axis, backward)  5.16 us
  transfers between devices with their start and end apart: 10, of which 9 were waited for; matrix products, arithmetic and copies ran while one was open for 3% of the time, Pallas kernels for 0%

commit v1 on v0

--- a/solution.py
+++ b/solution.py
@@ -133,7 +133,8 @@
     new_specimen = specimen + core_sum[0:2] / (core_sum[2:3] + 1.0)
     devices_count = lax.axis_size("scanx") * lax.axis_size("scany") * lax.axis_size("pos")
     step_size = 1.0 / math.sqrt(offsets.shape[0] * devices_count)
-    total_grad = lax.psum(probe_grad, ("scanx", "scany", "pos"))
+    parts = lax.all_gather(probe_grad, ("scanx", "scany", "pos"))
+    total_grad = jnp.sum(parts, axis=0)
     new_probe = probe_wave + total_grad * step_size
     return (new_specimen, new_probe)
 

time: 251 us -> 225 us (0.90)
  waiting for transfers between devices: 142 us -> 113 us
  other arithmetic: 29.9 us -> 32.8 us
    psum x1 -> x0, waiting for transfers between devices: 81.3 us -> none  [shards(): total_grad = lax.psum(probe_grad, ('scanx', 'scany', 'pos'))]
    all_gather x0 -> x1, waiting for transfers between devices: none -> 55.3 us  [shards(): parts = lax.all_gather(probe_grad, ('scanx', 'scany', 'pos'))]
    reduce_sum x0 -> x1, other arithmetic: none -> 4.03 us  [shards(): total_grad = jnp.sum(parts, axis=0)]
    psum x1, waiting for transfers between devices: 19.9 us -> 17 us  [shards(): core_sum = lax.psum(core_sum, 'pos')]
  transfers between devices with their start and end apart: 10 -> 10, of which waited for: 9 -> 9; matrix products, arithmetic and copies ran while one was open for 3% -> 4% of each run, Pallas kernels for 0% -> 0%
where the time goes in v1:
time: 225 us; the launch traced here: 224 us
  waiting for transfers between devices  113 us (50%)
  other arithmetic  32.8 us (15%)
  local copies, waits for them, and re-layouts  27.4 us (12%)
  starting transfers between devices  19.8 us (9%)
  between operations  15.7 us (7%)
  matrix products  7.75 us (3%)
  loops' own time  7.59 us (3%)
    all_gather x1, waiting for transfers between devices, shards(): parts = lax.all_gather(probe_grad, ('scanx', 'scany', 'pos'))  55.3 us
    ppermute x4, waiting for transfers between devices, padded_2(): lax.ppermute(lax.slice_in_dim(block, block.shape[dim] - width, None, axis...  26.5 us
    dynamic_update_slice x2, local copies, waits for them, and re-layouts, visit_position(): lax.dynamic_update_slice(object_grad, current + object_term, (zero_index,...  18.8 us
    psum x1, waiting for transfers between devices, shards(): core_sum = lax.psum(core_sum, 'pos')  17 us
    ppermute x4, starting transfers between devices, padded_2(): lax.ppermute(lax.slice_in_dim(block, block.shape[dim] - width, None, axis...  14.4 us
    ppermute x4, waiting for transfers between devices, padded_2(): lax.ppermute(lax.slice_in_dim(block, 0, width, axis=dim), axis, backward)  13.3 us
    another operation x1, loops' own time, shards(): lax.scan(visit_position, (start_grad, start_probe), (amplitudes, offsets))  7.59 us
    ppermute x4, starting transfers between devices, padded_2(): lax.ppermute(lax.slice_in_dim(block, 0, width, axis=dim), axis, backward)  5.29 us
  transfers between devices with their start and end apart: 10, of which 9 were waited for; matrix products, arithmetic and copies ran while one was open for 4% of the time, Pallas kernels for 0%

profile of v1, /device:TPU:0, one launch (start us, length us, event | category | flops | bytes accessed | tf_op | source)
XLA Modules:
  0.0 223.7 jit_solution(3575352932173154658)
XLA Ops:
  10.5 5.6 %collective-permute-start = (f32[2,128,256]{2,1,0:T(8,128)S(1)}, f32[2,128,256]{2,1,0:T(8,128)S(1)}, u32[]{:S(2)}, u32[]{:S(2)}) collective-permute-start(f32[2,128,256]{2,1,0:T(8,128)S(1)} %get-tuple-element.198), channel_id=1, source_target_pairs={{0,4},{4,8},{8,12},{1,5},{5,9},{9,13},{2,6},{6,10},{10,14},{3,7},{... | collective-permute-start | bytes 786440 | tf_op jit(solution)/shard_map/ppermute | solution.py:13
  19.1 2.5 %collective-permute-done = f32[2,128,256]{2,1,0:T(8,128)S(1)} collective-permute-done((f32[2,128,256]{2,1,0:T(8,128)S(1)}, f32[2,128,256]{2,1,0:T(8,128)S(1)}, u32[]{:S(2)}, u32[]{:S(2)}) %collective-permute-start) | collective-permute-done | bytes 262176 | tf_op jit(solution)/shard_map/ppermute | solution.py:13
  22.6 4.4 %collective-permute-start.2 = (f32[2,512,128]{2,1,0:T(8,128)}, f32[2,512,128]{2,1,0:T(8,128)}, u32[]{:S(2)}, u32[]{:S(2)}) collective-permute-start(f32[2,512,128]{2,1,0:T(8,128)} %get-tuple-element.193), channel_id=1, source_target_pairs={{0,2},{1,3},{4,6},{5,7},{8,10},{9,11},{12,14},{13,15},{16,18},{17,... | collective-permute-start | bytes 1572872 | tf_op jit(solution)/shard_map/ppermute | solution.py:13
  30.6 5.9 %collective-permute-done.2 = f32[2,512,128]{2,1,0:T(8,128)} collective-permute-done((f32[2,512,128]{2,1,0:T(8,128)}, f32[2,512,128]{2,1,0:T(8,128)}, u32[]{:S(2)}, u32[]{:S(2)}) %collective-permute-start.2) | collective-permute-done | bytes 524320 | tf_op jit(solution)/shard_map/ppermute | solution.py:13
  36.5 4.7 %collective-permute-done.3 = f32[2,512,128]{2,1,0:T(8,128)} collective-permute-done((f32[2,512,128]{2,1,0:T(8,128)S(1)}, f32[2,512,128]{2,1,0:T(8,128)}, u32[]{:S(2)}, u32[]{:S(2)}) %collective-permute-start.3) | collective-permute-done | bytes 524320 | tf_op jit(solution)/shard_map/ppermute | solution.py:16
  42.6 2.0 broadcast_in_dim.10
  44.6 53.8 %while.14 = (s32[]{:T(128)}, f32[3,512,512]{2,1,0:T(8,128)}, f32[2,256,256]{2,1,0:T(8,128)}, s32[2,2]{1,0:T(2,128)S(1)}, f32[256,256]{1,0:T(8,128)}, /*index=5*/...) while((s32[]{:T(128)}, f32[3,512,512]{2,1,0:T(8,128)}, ...), condition=%wide.region_1.2_spmd.clone, body=%wide.region_0.1_spmd.clone.sunk | while | flops 540737536 | bytes 17170760 | solution.py:125
  49.0 2.0 fusion.72
  54.6 2.0 convolution_bitcast_fusion.7
  61.6 9.5 %dynamic_update_slice.6 = f32[3,512,512]{2,1,0:T(8,128)} dynamic-update-slice(f32[3,512,512]{2,1,0:T(8,128)} %get-tuple-element.314, f32[3,256,256]{2,1,0:T(8,128)S(1)} %maximum_add_fusion.4, s32[]{:T(128)} %constant.40.clone.1..sunk, s32[]{:T(128)S(6)} %select_n.64, s32[]{:T(128)S(6)} %select_n.65) | dynamic-update-slice | bytes 1572868 | tf_op jit(solution)/shard_map/while/body/eval_jaxpr/dynamic_update_slice | solution.py:112
  75.4 2.0 fusion.72
  77.4 1.9 convolution_bitcast_fusion.6
  81.1 2.0 convolution_bitcast_fusion.7
  85.5 1.9 maximum_add_fusion.5
  89.1 9.4 %dynamic_update_slice.6 = f32[3,512,512]{2,1,0:T(8,128)} dynamic-update-slice(f32[3,512,512]{2,1,0:T(8,128)} %get-tuple-element.314, f32[3,256,256]{2,1,0:T(8,128)S(1)} %maximum_add_fusion.4, s32[]{:T(128)} %constant.40.clone.1..sunk, s32[]{:T(128)S(6)} %select_n.64, s32[]{:T(128)S(6)} %select_n.65) | dynamic-update-slice | bytes 1572868 | tf_op jit(solution)/shard_map/while/body/eval_jaxpr/dynamic_update_slice | solution.py:112
  100.1 3.0 %collective-permute-start.4 = (f32[3,128,512]{2,1,0:T(8,128)S(1)}, f32[3,128,512]{2,1,0:T(8,128)S(1)}, u32[]{:S(2)}, u32[]{:S(2)}) collective-permute-start(f32[3,128,512]{2,1,0:T(8,128)S(1)} %get-tuple-element.189), channel_id=1, source_target_pairs={{0,4},{4,8},{8,12},{1,5},{5,9},{9,13},{2,6},{6,10},{10,14},{3,7},{... | collective-permute-start | bytes 2359304 | tf_op jit(solution)/shard_map/ppermute | solution.py:13
  104.3 14.3 %collective-permute-done.4 = f32[3,128,512]{2,1,0:T(8,128)S(1)} collective-permute-done((f32[3,128,512]{2,1,0:T(8,128)S(1)}, f32[3,128,512]{2,1,0:T(8,128)S(1)}, u32[]{:S(2)}, u32[]{:S(2)}) %collective-permute-start.4) | collective-permute-done | bytes 786464 | tf_op jit(solution)/shard_map/ppermute | solution.py:13
  118.6 4.2 %collective-permute-done.5 = f32[3,128,512]{2,1,0:T(8,128)S(1)} collective-permute-done((f32[3,128,512]{2,1,0:T(8,128)S(1)}, f32[3,128,512]{2,1,0:T(8,128)S(1)}, u32[]{:S(2)}, u32[]{:S(2)}) %collective-permute-start.5) | collective-permute-done | bytes 786464 | tf_op jit(solution)/shard_map/ppermute | solution.py:16
  126.1 3.9 %collective-permute-done.6 = f32[3,256,128]{2,1,0:T(8,128)S(1)} collective-permute-done((f32[3,256,128]{2,1,0:T(8,128)S(1)}, f32[3,256,128]{2,1,0:T(8,128)S(1)}, u32[]{:S(2)}, u32[]{:S(2)}) %collective-permute-start.6) | collective-permute-done | bytes 393248 | tf_op jit(solution)/shard_map/ppermute | solution.py:13
  130.1 4.4 %collective-permute-done.7 = f32[3,256,128]{2,1,0:T(8,128)S(1)} collective-permute-done((f32[3,256,128]{2,1,0:T(8,128)S(1)}, f32[3,256,128]{2,1,0:T(8,128)S(1)}, u32[]{:S(2)}, u32[]{:S(2)}) %collective-permute-start.7) | collective-permute-done | bytes 393248 | tf_op jit(solution)/shard_map/ppermute | solution.py:16
  136.2 17.0 %all-reduce.6.cloned.1.call-done = f32[3,256,256]{2,1,0:T(8,128)} async-done(((f32[3,256,256]{2,1,0:T(8,128)}), f32[3,256,256]{2,1,0:T(8,128)}) %all-reduce.6.cloned.1.call-update) | async-done | bytes 786448 | tf_op jit(solution)/shard_map/psum | solution.py:132
  154.2 1.9 fusion.29
  156.1 55.3 %all-gather.3.cloned.1.call-done = f32[32,256,256]{2,1,0:T(8,128)} async-done(((f32[2,256,256]{2,1,0:T(8,128)}), f32[32,256,256]{2,1,0:T(8,128)}) %all-gather.3.cloned.1.call-update) | async-done | bytes 8388624 | tf_op jit(solution)/shard_map/all_gather | solution.py:136
  211.4 4.0 %reduce_sum.9 = f32[2,256,256]{2,1,0:T(8,128)S(1)} reduce(f32[16,2,256,256]{3,2,1,0:T(8,128)} %bitcast.152, f32[]{:T(128)} %constant.41.clone.1), dimensions={0}, to_apply=%region_3.4 | reduce | flops 1966080 | bytes 8912900 | tf_op jit(solution)/shard_map/reduce_sum | solution.py:137
  (57 shorter events, 36.9 us)
Async XLA Ops:
  8.0 13.6 %copy-start.1 = (f32[2,256,256]{2,1,0:T(8,128)S(1)}, f32[2,256,256]{2,1,0:T(8,128)}, u32[]{:S(2)}) copy-start(f32[2,256,256]{2,1,0:T(8,128)} %param.6) | copy-start | bytes 1572868
  8.0 145.2 %all-reduce.6.cloned.1.call-start = ((), (), s32[]{:S(2)}) async-start(), calls=%async_computation | async-start | bytes 1572864 | tf_op jit(solution)/shard_map/psum | solution.py:132
  9.2 12.5 %collective-permute-start.1 = (f32[2,128,256]{2,1,0:T(8,128)S(1)}, f32[2,128,256]{2,1,0:T(8,128)S(1)}, u32[]{:S(2)}, u32[]{:S(2)}) collective-permute-start(f32[2,128,256]{2,1,0:T(8,128)S(1)} %get-tuple-element.197), channel_id=1, source_target_pairs={{4,0},{8,4},{12,8},{5,1},{9,5},{13,9},{6,2},{10,6},{14,10},{7,3},{... | collective-permute-start | bytes 786440 | tf_op jit(solution)/shard_map/ppermute | solution.py:16
  10.5 11.1 %collective-permute-start = (f32[2,128,256]{2,1,0:T(8,128)S(1)}, f32[2,128,256]{2,1,0:T(8,128)S(1)}, u32[]{:S(2)}, u32[]{:S(2)}) collective-permute-start(f32[2,128,256]{2,1,0:T(8,128)S(1)} %get-tuple-element.198), channel_id=1, source_target_pairs={{0,4},{4,8},{8,12},{1,5},{5,9},{9,13},{2,6},{6,10},{10,14},{3,7},{... | collective-permute-start | bytes 786440 | tf_op jit(solution)/shard_map/ppermute | solution.py:13
  21.7 7.4 %copy-start.3 = (f32[2,256,256]{2,1,0:T(8,128)S(1)}, f32[2,256,256]{2,1,0:T(8,128)}, u32[]{:S(2)}) copy-start(f32[2,256,256]{2,1,0:T(8,128)} %param.7) | copy-start | bytes 1572868
  22.6 13.9 %collective-permute-start.2 = (f32[2,512,128]{2,1,0:T(8,128)}, f32[2,512,128]{2,1,0:T(8,128)}, u32[]{:S(2)}, u32[]{:S(2)}) collective-permute-start(f32[2,512,128]{2,1,0:T(8,128)} %get-tuple-element.193), channel_id=1, source_target_pairs={{0,2},{1,3},{4,6},{5,7},{8,10},{9,11},{12,14},{13,15},{16,18},{17,... | collective-permute-start | bytes 1572872 | tf_op jit(solution)/shard_map/ppermute | solution.py:13
  27.0 14.2 %collective-permute-start.3 = (f32[2,512,128]{2,1,0:T(8,128)S(1)}, f32[2,512,128]{2,1,0:T(8,128)}, u32[]{:S(2)}, u32[]{:S(2)}) collective-permute-start(f32[2,512,128]{2,1,0:T(8,128)S(1)} %get-tuple-element.194), channel_id=1, source_target_pairs={{2,0},{3,1},{6,4},{7,5},{10,8},{11,9},{14,12},{15,13},{18,16},{19,... | collective-permute-start | bytes 1572872 | tf_op jit(solution)/shard_map/ppermute | solution.py:16
  42.6 2.0 copy-start.5
  98.4 24.3 %copy-start = (f32[3,512,512]{2,1,0:T(8,128)S(1)}, f32[3,512,512]{2,1,0:T(8,128)}, u32[]{:S(2)}) copy-start(f32[3,512,512]{2,1,0:T(8,128)} %get-tuple-element.93) | copy-start | bytes 9437188
  100.1 18.5 %collective-permute-start.4 = (f32[3,128,512]{2,1,0:T(8,128)S(1)}, f32[3,128,512]{2,1,0:T(8,128)S(1)}, u32[]{:S(2)}, u32[]{:S(2)}) collective-permute-start(f32[3,128,512]{2,1,0:T(8,128)S(1)} %get-tuple-element.189), channel_id=1, source_target_pairs={{0,4},{4,8},{8,12},{1,5},{5,9},{9,13},{2,6},{6,10},{10,14},{3,7},{... | collective-permute-start | bytes 2359304 | tf_op jit(solution)/shard_map/ppermute | solution.py:13
  103.0 19.7 %collective-permute-start.5 = (f32[3,128,512]{2,1,0:T(8,128)S(1)}, f32[3,128,512]{2,1,0:T(8,128)S(1)}, u32[]{:S(2)}, u32[]{:S(2)}) collective-permute-start(f32[3,128,512]{2,1,0:T(8,128)S(1)} %get-tuple-element.190), channel_id=1, source_target_pairs={{4,0},{8,4},{12,8},{5,1},{9,5},{13,9},{6,2},{10,6},{14,10},{7,3},{... | collective-permute-start | bytes 2359304 | tf_op jit(solution)/shard_map/ppermute | solution.py:16
  123.2 6.9 %collective-permute-start.6 = (f32[3,256,128]{2,1,0:T(8,128)S(1)}, f32[3,256,128]{2,1,0:T(8,128)S(1)}, u32[]{:S(2)}, u32[]{:S(2)}) collective-permute-start(f32[3,256,128]{2,1,0:T(8,128)S(1)} %get-tuple-element.191), channel_id=1, source_target_pairs={{0,2},{1,3},{4,6},{5,7},{8,10},{9,11},{12,14},{13,15},{16,18},{17,... | collective-permute-start | bytes 1179656 | tf_op jit(solution)/shard_map/ppermute | solution.py:13
  124.7 29.5 %copy-start.2 = (f32[2,256,256]{2,1,0:T(8,128)S(1)}, f32[2,256,256]{2,1,0:T(8,128)}, u32[]{:S(2)}) copy-start(f32[2,256,256]{2,1,0:T(8,128)} %param.6) | copy-start | bytes 1572868
  124.7 9.8 %collective-permute-start.7 = (f32[3,256,128]{2,1,0:T(8,128)S(1)}, f32[3,256,128]{2,1,0:T(8,128)S(1)}, u32[]{:S(2)}, u32[]{:S(2)}) collective-permute-start(f32[3,256,128]{2,1,0:T(8,128)S(1)} %get-tuple-element.192), channel_id=1, source_target_pairs={{2,0},{3,1},{6,4},{7,5},{10,8},{11,9},{14,12},{15,13},{18,16},{19,... | collective-permute-start | bytes 1179656 | tf_op jit(solution)/shard_map/ppermute | solution.py:16
  135.6 75.8 %all-gather.3.cloned.1.call-start = ((), (), s32[]{:S(2)}) async-start(), calls=%async_computation.1 | async-start | bytes 8912896 | tf_op jit(solution)/shard_map/all_gather | solution.py:136
  211.4 4.0 %copy-start.4 = (f32[2,256,256]{2,1,0:T(8,128)S(1)}, f32[2,256,256]{2,1,0:T(8,128)}, u32[]{:S(2)}) copy-start(f32[2,256,256]{2,1,0:T(8,128)} %param.7) | copy-start | bytes 1572868
Sparse Core Ops, SparseCore 0:
  135.7 17.4 all-reduce.5
Sparse Core Ops, SparseCore 1:
  138.8 72.5 all-gather.2
